TPU v7x, 256 devices: a whole 4x4x8 slice. The times are simulated.
256 devices in a mesh: segment: 4 (over y), blk: 64 (over x, z, core).
Axes of the slice: x: 4, y: 4, z: 8, core: 2. Of those that a mesh axis runs over, the one named last changes fastest.
Arguments:
- inputs: bfloat16 [4, 1024, 64, 128], P(None, 'blk'), may hold values from -6 to 6
- weights: bfloat16 [8, 1024, 64, 2048], P('segment', 'blk'), may hold values from -0.1875 to 0.1875
- biases: float32 [8, 1024, 64], P('segment', 'blk'), may hold values from -3 to 3
- tile_index: int32 [8, 1024, 32], P('segment', 'blk'), may hold values from 0 to 31, each once within a row
Outputs:
- final_activity: bfloat16 [4, 1024, 64, 128], P('segment', 'blk')
Inputs may be any that keep to these rules, and one draw needn't show every extreme that they name: `tile_index`: each row of 32 entries names every member 0..31 once.
All inputs are finite; a program needn't handle non-finite values.
Results may differ from a plain program's by a relative error of at most 0.014.
Values may be sent and summed in bfloat16 or wider, within the bound.
A program may use at most 128 MiB of HBM per device.

v0:
```python
import jax
import jax.numpy as jnp
from jax import lax
from jax.sharding import PartitionSpec as P


def from_partner(array, axis, stride):
    return lax.ppermute(array, axis, [(i, i ^ 1 << stride) for i in range(lax.axis_size(axis))])


def passed_along(value, axis, steps):
    count = lax.axis_size(axis)
    initial, last = (max(0, -steps), min(count, count - steps))
    return lax.ppermute(value, axis, [(source, source + steps) for source in range(initial, last)])


def permuted_weights(weights, tile_index):
    blocks, tile_size, row_width = weights.shape
    fan_count = tile_index.shape[1]
    shaped = weights.reshape(blocks, tile_size, fan_count, row_width // fan_count)
    onehot = (
        tile_index[:, :, None] == jnp.arange(fan_count, dtype=jnp.int32)[None, None, :]
    ).astype(jnp.bfloat16)
    placed = jnp.einsum("jakc,jkm->jamc", shaped, onehot, preferred_element_type=jnp.float32)
    return placed.astype(jnp.bfloat16).reshape(blocks * tile_size, row_width)


def join_group(activity, bit_place):
    partner = from_partner(activity, "blk", bit_place)
    upper_half = lax.axis_index("blk") // (1 << bit_place) % 2
    first_order = jnp.concatenate([activity, partner], axis=0)
    second = jnp.concatenate([partner, activity], axis=0)
    return jnp.where(upper_half == 0, first_order, second)


def apply_layer(activity, bit_place, matrix, offset):
    grouped = join_group(activity, bit_place)
    members, tile_size, batch_size = grouped.shape
    flat_group = grouped.reshape(members * tile_size, batch_size)
    summed = jnp.dot(matrix, flat_group, preferred_element_type=jnp.float32)
    summed = summed.reshape(activity.shape) + offset[:, :, None]
    return jnp.maximum(summed, 0.0).astype(jnp.bfloat16)


def regroup_segmented(activity, group_size):
    local_blocks, tile_size, batch_size = activity.shape
    position = lax.axis_index("blk")
    for level_index in range(group_size.bit_length() - 1):
        shaped = activity.reshape(
            local_blocks >> level_index + 1, 2, 1 << level_index, tile_size, batch_size
        )
        own_bit = (position >> level_index + 1) % 2
        outgoing = lax.dynamic_index_in_dim(shaped, 1 - own_bit, 1, keepdims=True)
        incoming = from_partner(outgoing, "blk", level_index + 1)
        shaped = lax.dynamic_update_index_in_dim(shaped, incoming, 1 - own_bit, 1)
        activity = shaped.reshape(local_blocks, tile_size, batch_size)
    return activity


def body(inputs, weights, biases, tile_index):
    segments = lax.axis_size("segment")
    segment_index = lax.axis_index("segment")
    devices = lax.axis_size("blk")
    local_blocks = inputs.shape[1]
    group_size = min(local_blocks, devices // 4)
    far_bit = (2 * group_size).bit_length() - 1
    micro_count = inputs.shape[0]
    matrices = [
        permuted_weights(weights[layer_index], tile_index[layer_index]) for layer_index in range(2)
    ]
    results = jnp.zeros(inputs.shape, jnp.bfloat16)
    arriving = jnp.zeros(inputs.shape[1:], jnp.bfloat16)
    step_count = micro_count + segments - 1
    for step_index in range(step_count):
        new_input = inputs[min(step_index, micro_count - 1)]
        present = jnp.where(segment_index == 0, new_input, arriving)
        present = apply_layer(present, 0, matrices[0], biases[0])
        present = regroup_segmented(present, group_size)
        present = apply_layer(present, far_bit, matrices[1], biases[1])
        present = regroup_segmented(present, group_size)
        finished = step_index - (segments - 1)
        if finished >= 0:
            results = results.at[finished].set(present)
        if step_index + 1 < step_count:
            arriving = passed_along(present, "segment", 1)
    gathered = lax.all_to_all(results[:, None], "segment", split_axis=0, concat_axis=1, tiled=True)
    return gathered[:, segments - 1]


def solution(mesh):
    in_specs = (
        P(None, "blk", None, None),
        P("segment", "blk", None, None),
        P("segment", "blk", None),
        P("segment", "blk", None),
    )
    out_specs = P("segment", "blk", None, None)
    return jax.shard_map(body, mesh=mesh, in_specs=in_specs, out_specs=out_specs, check_vma=False)
```

profile of v0, /device:TPU:96, one launch (start us, length us, event | category | flops | bytes accessed | tf_op | source)
XLA Modules:
  0.0 690.5 jit_solution(18264248735898804815)
XLA Ops:
  7.4 12.9 %reshape_squeeze.7 = bf16[16,64,32,64]{3,2,1,0:T(8,128)(2,1)} reshape(bf16[1,16,64,2048]{3,2,1,0:T(8,128)(2,1)} %get-tuple-element.53) | data formatting | bytes 8388608 | tf_op jit(solution)/shard_map/reshape;squeeze | solution.py:20
  20.3 9.1 %convert_bitcast_fusion = bf16[16,64,32,64]{3,2,1,0:T(8,128)(2,1)} fusion(bf16[16,64,32,64]{3,2,1,0:T(8,128)(2,1)} %reshape_squeeze.7, s32[16,32]{1,0:T(8,128)S(1)} %get-tuple-element.57), kind=kOutput, calls=%fused_computation | convolution fusion | flops 136331264 | bytes 8390656 | tf_op jit(solution)/shard_map/jakc,jkm->jamc/dot_general | solution.py:24
  29.3 9.2 %fusion.163 = bf16[16,64,128]{2,1,0:T(8,128)(2,1)S(1)} fusion(bf16[16,64,32,64]{3,2,1,0:T(8,128)(2,1)} %convert_bitcast_fusion, bf16[16,64,128]{2,1,0:T(8,128)(2,1)S(1)} %collective-permute-done, bf16[16,64,128]{2,1,0:T(8,128)(2,1)S(1)} %select_bitcast_fusion, pred[]{:T(512)S(6)} %eq.137, f32[16,64]{1,0:T(8,128)S(1)} %get-tuple-element.56), kind=kOutput, calls=%fused_computation.75 | convolution fusion | flops 538050560 | bytes 4984833 | tf_op jit(solution)/shard_map/dot_general | solution.py:40
  44.7 8.6 %collective-permute-done.2 = bf16[4,1,2,64,128]{4,3,2,1,0:T(8,128)(2,1)S(1)} collective-permute-done((bf16[4,1,2,64,128]{4,3,2,1,0:T(8,128)(2,1)S(1)}, bf16[4,1,2,64,128]{4,3,2,1,0:T(8,128)(2,1)S(1)}, u32[]{:S(2)}, u32[]{:S(2)}) %collective-permute-start.2) | collective-permute-done | bytes 131104 | tf_op jit(solution)/shard_map/ppermute | solution.py:8
  58.2 7.5 %collective-permute-done.3 = bf16[2,1,4,64,128]{4,3,2,1,0:T(8,128)(2,1)S(1)} collective-permute-done((bf16[2,1,4,64,128]{4,3,2,1,0:T(8,128)(2,1)S(1)}, bf16[2,1,4,64,128]{4,3,2,1,0:T(8,128)(2,1)S(1)}, u32[]{:S(2)}, u32[]{:S(2)}) %collective-permute-start.3) | collective-permute-done | bytes 131104 | tf_op jit(solution)/shard_map/ppermute | solution.py:8
  67.4 12.9 %reshape_squeeze.6 = bf16[16,64,32,64]{3,2,1,0:T(8,128)(2,1)} reshape(bf16[1,16,64,2048]{3,2,1,0:T(8,128)(2,1)} %get-tuple-element.54) | data formatting | bytes 8388608 | tf_op jit(solution)/shard_map/reshape;squeeze | solution.py:20
  83.1 9.0 %convert_bitcast_fusion.1 = bf16[16,64,32,64]{3,2,1,0:T(8,128)(2,1)} fusion(bf16[16,64,32,64]{3,2,1,0:T(8,128)(2,1)} %reshape_squeeze.6, s32[16,32]{1,0:T(8,128)S(1)} %get-tuple-element.58), kind=kOutput, calls=%fused_computation.1 | convolution fusion | flops 136331264 | bytes 8390656 | tf_op jit(solution)/shard_map/jakc,jkm->jamc/dot_general | solution.py:24
  92.1 9.2 %fusion.184 = bf16[16,64,128]{2,1,0:T(8,128)(2,1)S(1)} fusion(bf16[16,64,32,64]{3,2,1,0:T(8,128)(2,1)} %convert_bitcast_fusion.1, bf16[16,64,128]{2,1,0:T(8,128)(2,1)S(1)} %collective-permute-done.5, bf16[16,64,128]{2,1,0:T(8,128)(2,1)S(1)} %bitcast.344, pred[]{:T(512)S(6)} %eq.132, f32[16,64]{1,0:T(8,128)S(1)} %get-tuple-element.55), kind=kOutput, calls=%fused_computation.82 | convolution fusion | flops 538050560 | bytes 4984833 | tf_op jit(solution)/shard_map/dot_general | solution.py:40
  137.5 10.0 %fusion.160 = bf16[16,64,128]{2,1,0:T(8,128)(2,1)S(1)} fusion(bf16[16,64,32,64]{3,2,1,0:T(8,128)(2,1)} %convert_bitcast_fusion, bf16[16,64,128]{2,1,0:T(8,128)(2,1)S(1)} %collective-permute-done.11, bf16[16,64,128]{2,1,0:T(8,128)(2,1)S(1)} %bitcast_select_fusion, pred[]{:T(512)S(6)} %eq.137, f32[16,64]{1,0:T(8,128)S(1)} %get-tuple-element.56), kind=kOutput, calls=%fused_computation.74 | convolution fusion | flops 538050560 | bytes 4984833 | tf_op jit(solution)/shard_map/dot_general | solution.py:40
  152.9 7.2 %collective-permute-done.13 = bf16[4,1,2,64,128]{4,3,2,1,0:T(8,128)(2,1)S(1)} collective-permute-done((bf16[4,1,2,64,128]{4,3,2,1,0:T(8,128)(2,1)S(1)}, bf16[4,1,2,64,128]{4,3,2,1,0:T(8,128)(2,1)S(1)}, u32[]{:S(2)}, u32[]{:S(2)}) %collective-permute-start.13) | collective-permute-done | bytes 131104 | tf_op jit(solution)/shard_map/ppermute | solution.py:8
  163.5 7.9 %collective-permute-done.14 = bf16[2,1,4,64,128]{4,3,2,1,0:T(8,128)(2,1)S(1)} collective-permute-done((bf16[2,1,4,64,128]{4,3,2,1,0:T(8,128)(2,1)S(1)}, bf16[2,1,4,64,128]{4,3,2,1,0:T(8,128)(2,1)S(1)}, u32[]{:S(2)}, u32[]{:S(2)}) %collective-permute-start.14) | collective-permute-done | bytes 131104 | tf_op jit(solution)/shard_map/ppermute | solution.py:8
  177.9 7.8 %collective-permute-done.16 = bf16[16,64,128]{2,1,0:T(8,128)(2,1)S(1)} collective-permute-done((bf16[16,64,128]{2,1,0:T(8,128)(2,1)S(1)}, bf16[16,64,128]{2,1,0:T(8,128)(2,1)S(1)}, u32[]{:S(2)}, u32[]{:S(2)}) %collective-permute-start.16) | collective-permute-done | bytes 262176 | tf_op jit(solution)/shard_map/ppermute | solution.py:8
  241.6 8.4 %collective-permute-done.24 = bf16[4,1,2,64,128]{4,3,2,1,0:T(8,128)(2,1)S(1)} collective-permute-done((bf16[4,1,2,64,128]{4,3,2,1,0:T(8,128)(2,1)S(1)}, bf16[4,1,2,64,128]{4,3,2,1,0:T(8,128)(2,1)S(1)}, u32[]{:S(2)}, u32[]{:S(2)}) %collective-permute-start.24) | collective-permute-done | bytes 131104 | tf_op jit(solution)/shard_map/ppermute | solution.py:8
  253.1 8.8 %collective-permute-done.25 = bf16[2,1,4,64,128]{4,3,2,1,0:T(8,128)(2,1)S(1)} collective-permute-done((bf16[2,1,4,64,128]{4,3,2,1,0:T(8,128)(2,1)S(1)}, bf16[2,1,4,64,128]{4,3,2,1,0:T(8,128)(2,1)S(1)}, u32[]{:S(2)}, u32[]{:S(2)}) %collective-permute-start.25) | collective-permute-done | bytes 131104 | tf_op jit(solution)/shard_map/ppermute | solution.py:8
  268.5 8.1 %collective-permute-done.27 = bf16[16,64,128]{2,1,0:T(8,128)(2,1)S(1)} collective-permute-done((bf16[16,64,128]{2,1,0:T(8,128)(2,1)S(1)}, bf16[16,64,128]{2,1,0:T(8,128)(2,1)S(1)}, u32[]{:S(2)}, u32[]{:S(2)}) %collective-permute-start.27) | collective-permute-done | bytes 262176 | tf_op jit(solution)/shard_map/ppermute | solution.py:8
  297.9 7.3 %collective-permute-done.30 = bf16[2,1,4,64,128]{4,3,2,1,0:T(8,128)(2,1)S(1)} collective-permute-done((bf16[2,1,4,64,128]{4,3,2,1,0:T(8,128)(2,1)S(1)}, bf16[2,1,4,64,128]{4,3,2,1,0:T(8,128)(2,1)S(1)}, u32[]{:S(2)}, u32[]{:S(2)}) %collective-permute-start.30) | collective-permute-done | bytes 131104 | tf_op jit(solution)/shard_map/ppermute | solution.py:8
  332.5 8.4 %collective-permute-done.35 = bf16[4,1,2,64,128]{4,3,2,1,0:T(8,128)(2,1)S(1)} collective-permute-done((bf16[4,1,2,64,128]{4,3,2,1,0:T(8,128)(2,1)S(1)}, bf16[4,1,2,64,128]{4,3,2,1,0:T(8,128)(2,1)S(1)}, u32[]{:S(2)}, u32[]{:S(2)}) %collective-permute-start.35) | collective-permute-done | bytes 131104 | tf_op jit(solution)/shard_map/ppermute | solution.py:8
  344.0 8.8 %collective-permute-done.36 = bf16[2,1,4,64,128]{4,3,2,1,0:T(8,128)(2,1)S(1)} collective-permute-done((bf16[2,1,4,64,128]{4,3,2,1,0:T(8,128)(2,1)S(1)}, bf16[2,1,4,64,128]{4,3,2,1,0:T(8,128)(2,1)S(1)}, u32[]{:S(2)}, u32[]{:S(2)}) %collective-permute-start.36) | collective-permute-done | bytes 131104 | tf_op jit(solution)/shard_map/ppermute | solution.py:8
  359.4 8.1 %collective-permute-done.38 = bf16[16,64,128]{2,1,0:T(8,128)(2,1)S(1)} collective-permute-done((bf16[16,64,128]{2,1,0:T(8,128)(2,1)S(1)}, bf16[16,64,128]{2,1,0:T(8,128)(2,1)S(1)}, u32[]{:S(2)}, u32[]{:S(2)}) %collective-permute-start.38) | collective-permute-done | bytes 262176 | tf_op jit(solution)/shard_map/ppermute | solution.py:8
  388.7 7.3 %collective-permute-done.41 = bf16[2,1,4,64,128]{4,3,2,1,0:T(8,128)(2,1)S(1)} collective-permute-done((bf16[2,1,4,64,128]{4,3,2,1,0:T(8,128)(2,1)S(1)}, bf16[2,1,4,64,128]{4,3,2,1,0:T(8,128)(2,1)S(1)}, u32[]{:S(2)}, u32[]{:S(2)}) %collective-permute-start.41) | collective-permute-done | bytes 131104 | tf_op jit(solution)/shard_map/ppermute | solution.py:8
  423.2 8.4 %collective-permute-done.46 = bf16[4,1,2,64,128]{4,3,2,1,0:T(8,128)(2,1)S(1)} collective-permute-done((bf16[4,1,2,64,128]{4,3,2,1,0:T(8,128)(2,1)S(1)}, bf16[4,1,2,64,128]{4,3,2,1,0:T(8,128)(2,1)S(1)}, u32[]{:S(2)}, u32[]{:S(2)}) %collective-permute-start.46) | collective-permute-done | bytes 131104 | tf_op jit(solution)/shard_map/ppermute | solution.py:8
  434.7 8.8 %collective-permute-done.47 = bf16[2,1,4,64,128]{4,3,2,1,0:T(8,128)(2,1)S(1)} collective-permute-done((bf16[2,1,4,64,128]{4,3,2,1,0:T(8,128)(2,1)S(1)}, bf16[2,1,4,64,128]{4,3,2,1,0:T(8,128)(2,1)S(1)}, u32[]{:S(2)}, u32[]{:S(2)}) %collective-permute-start.47) | collective-permute-done | bytes 131104 | tf_op jit(solution)/shard_map/ppermute | solution.py:8
  450.3 8.1 %collective-permute-done.49 = bf16[16,64,128]{2,1,0:T(8,128)(2,1)S(1)} collective-permute-done((bf16[16,64,128]{2,1,0:T(8,128)(2,1)S(1)}, bf16[16,64,128]{2,1,0:T(8,128)(2,1)S(1)}, u32[]{:S(2)}, u32[]{:S(2)}) %collective-permute-start.49) | collective-permute-done | bytes 262176 | tf_op jit(solution)/shard_map/ppermute | solution.py:8
  479.6 7.3 %collective-permute-done.52 = bf16[2,1,4,64,128]{4,3,2,1,0:T(8,128)(2,1)S(1)} collective-permute-done((bf16[2,1,4,64,128]{4,3,2,1,0:T(8,128)(2,1)S(1)}, bf16[2,1,4,64,128]{4,3,2,1,0:T(8,128)(2,1)S(1)}, u32[]{:S(2)}, u32[]{:S(2)}) %collective-permute-start.52) | collective-permute-done | bytes 131104 | tf_op jit(solution)/shard_map/ppermute | solution.py:8
  514.1 8.4 %collective-permute-done.57 = bf16[4,1,2,64,128]{4,3,2,1,0:T(8,128)(2,1)S(1)} collective-permute-done((bf16[4,1,2,64,128]{4,3,2,1,0:T(8,128)(2,1)S(1)}, bf16[4,1,2,64,128]{4,3,2,1,0:T(8,128)(2,1)S(1)}, u32[]{:S(2)}, u32[]{:S(2)}) %collective-permute-start.57) | collective-permute-done | bytes 131104 | tf_op jit(solution)/shard_map/ppermute | solution.py:8
  525.6 8.8 %collective-permute-done.58 = bf16[2,1,4,64,128]{4,3,2,1,0:T(8,128)(2,1)S(1)} collective-permute-done((bf16[2,1,4,64,128]{4,3,2,1,0:T(8,128)(2,1)S(1)}, bf16[2,1,4,64,128]{4,3,2,1,0:T(8,128)(2,1)S(1)}, u32[]{:S(2)}, u32[]{:S(2)}) %collective-permute-start.58) | collective-permute-done | bytes 131104 | tf_op jit(solution)/shard_map/ppermute | solution.py:8
  541.0 8.1 %collective-permute-done.60 = bf16[16,64,128]{2,1,0:T(8,128)(2,1)S(1)} collective-permute-done((bf16[16,64,128]{2,1,0:T(8,128)(2,1)S(1)}, bf16[16,64,128]{2,1,0:T(8,128)(2,1)S(1)}, u32[]{:S(2)}, u32[]{:S(2)}) %collective-permute-start.60) | collective-permute-done | bytes 262176 | tf_op jit(solution)/shard_map/ppermute | solution.py:8
  570.3 7.3 %collective-permute-done.63 = bf16[2,1,4,64,128]{4,3,2,1,0:T(8,128)(2,1)S(1)} collective-permute-done((bf16[2,1,4,64,128]{4,3,2,1,0:T(8,128)(2,1)S(1)}, bf16[2,1,4,64,128]{4,3,2,1,0:T(8,128)(2,1)S(1)}, u32[]{:S(2)}, u32[]{:S(2)}) %collective-permute-start.63) | collective-permute-done | bytes 131104 | tf_op jit(solution)/shard_map/ppermute | solution.py:8
  605.0 8.4 %collective-permute-done.68 = bf16[4,1,2,64,128]{4,3,2,1,0:T(8,128)(2,1)S(1)} collective-permute-done((bf16[4,1,2,64,128]{4,3,2,1,0:T(8,128)(2,1)S(1)}, bf16[4,1,2,64,128]{4,3,2,1,0:T(8,128)(2,1)S(1)}, u32[]{:S(2)}, u32[]{:S(2)}) %collective-permute-start.68) | collective-permute-done | bytes 131104 | tf_op jit(solution)/shard_map/ppermute | solution.py:8
  616.5 8.8 %collective-permute-done.69 = bf16[2,1,4,64,128]{4,3,2,1,0:T(8,128)(2,1)S(1)} collective-permute-done((bf16[2,1,4,64,128]{4,3,2,1,0:T(8,128)(2,1)S(1)}, bf16[2,1,4,64,128]{4,3,2,1,0:T(8,128)(2,1)S(1)}, u32[]{:S(2)}, u32[]{:S(2)}) %collective-permute-start.69) | collective-permute-done | bytes 131104 | tf_op jit(solution)/shard_map/ppermute | solution.py:8
  631.8 8.1 %collective-permute-done.71 = bf16[16,64,128]{2,1,0:T(8,128)(2,1)S(1)} collective-permute-done((bf16[16,64,128]{2,1,0:T(8,128)(2,1)S(1)}, bf16[16,64,128]{2,1,0:T(8,128)(2,1)S(1)}, u32[]{:S(2)}, u32[]{:S(2)}) %collective-permute-start.71) | collective-permute-done | bytes 262176 | tf_op jit(solution)/shard_map/ppermute | solution.py:8
  673.6 15.9 %all_to_all.12 = bf16[4,1,16,64,128]{4,3,2,1,0:T(8,128)(2,1)S(1)} all-to-all(bf16[4,1,16,64,128]{4,3,2,1,0:T(8,128)(2,1)S(1)} %bitcast_dynamic-update-slice_fusion), channel_id=1, replica_groups=mesh['segment'=4,'blk'=64] {'segment'}, dimensions={0} | all-to-all | bytes 2097152 | tf_op jit(solution)/shard_map/all_to_all | solution.py:86
  (282 shorter events, 406.9 us)
Async XLA Ops:
  1.0 28.4 %collective-permute-start = (bf16[16,64,128]{2,1,0:T(8,128)(2,1)S(1)}, bf16[16,64,128]{2,1,0:T(8,128)(2,1)S(1)}, u32[]{:S(2)}, u32[]{:S(2)}) collective-permute-start(bf16[16,64,128]{2,1,0:T(8,128)(2,1)S(1)} %select_bitcast_fusion), channel_id=1, source_target_pairs={{0,1},{1,0},{2,3},{3,2},{4,5},{5,4},{6,7},{7,6},{8,9},{9,8},{10,11... | collective-permute-start | bytes 786440 | tf_op jit(solution)/shard_map/ppermute | solution.py:8
  44.6 8.7 %collective-permute-start.2 = (bf16[4,1,2,64,128]{4,3,2,1,0:T(8,128)(2,1)S(1)}, bf16[4,1,2,64,128]{4,3,2,1,0:T(8,128)(2,1)S(1)}, u32[]{:S(2)}, u32[]{:S(2)}) collective-permute-start(bf16[4,1,2,64,128]{4,3,2,1,0:T(8,128)(2,1)S(1)} %constant_dynamic-slice_fusion.54), channel_id=1, source_target_pairs={{0,4},{1,5},{2,6},{3,7},{4,0},{5,1},{6,2},{7,3},{8,12},{9,13},{10,... | collective-permute-start | bytes 393224 | tf_op jit(solution)/shard_map/ppermute | solution.py:8
  53.4 12.4 %collective-permute-start.3 = (bf16[2,1,4,64,128]{4,3,2,1,0:T(8,128)(2,1)S(1)}, bf16[2,1,4,64,128]{4,3,2,1,0:T(8,128)(2,1)S(1)}, u32[]{:S(2)}, u32[]{:S(2)}) collective-permute-start(bf16[2,1,4,64,128]{4,3,2,1,0:T(8,128)(2,1)S(1)} %constant_dynamic-slice_fusion.53), channel_id=1, source_target_pairs={{0,8},{1,9},{2,10},{3,11},{4,12},{5,13},{6,14},{7,15},{8,0},{9,1},... | collective-permute-start | bytes 393224 | tf_op jit(solution)/shard_map/ppermute | solution.py:8
  65.8 14.4 %collective-permute-start.4 = (bf16[1,1,8,64,128]{4,3,2,1,0:T(8,128)(2,1)S(1)}, bf16[1,1,8,64,128]{4,3,2,1,0:T(8,128)(2,1)S(1)}, u32[]{:S(2)}, u32[]{:S(2)}) collective-permute-start(bf16[1,1,8,64,128]{4,3,2,1,0:T(8,128)(2,1)S(1)} %constant_dynamic-slice_fusion.52), channel_id=1, source_target_pairs={{0,16},{1,17},{2,18},{3,19},{4,20},{5,21},{6,22},{7,23},{8,24},{9,... | collective-permute-start | bytes 393224 | tf_op jit(solution)/shard_map/ppermute | solution.py:8
  80.2 11.9 %collective-permute-start.5 = (bf16[16,64,128]{2,1,0:T(8,128)(2,1)S(1)}, bf16[16,64,128]{2,1,0:T(8,128)(2,1)S(1)}, u32[]{:S(2)}, u32[]{:S(2)}) collective-permute-start(bf16[16,64,128]{2,1,0:T(8,128)(2,1)S(1)} %bitcast.343), channel_id=1, source_target_pairs={{0,32},{1,33},{2,34},{3,35},{4,36},{5,37},{6,38},{7,39},{8,40},{9,... | collective-permute-start | bytes 786440 | tf_op jit(solution)/shard_map/ppermute | solution.py:8
  113.5 9.8 %collective-permute-start.8 = (bf16[2,1,4,64,128]{4,3,2,1,0:T(8,128)(2,1)S(1)}, bf16[2,1,4,64,128]{4,3,2,1,0:T(8,128)(2,1)S(1)}, u32[]{:S(2)}, u32[]{:S(2)}) collective-permute-start(bf16[2,1,4,64,128]{4,3,2,1,0:T(8,128)(2,1)S(1)} %constant_dynamic-slice_fusion.49), channel_id=1, source_target_pairs={{0,8},{1,9},{2,10},{3,11},{4,12},{5,13},{6,14},{7,15},{8,0},{9,1},... | collective-permute-start | bytes 393224 | tf_op jit(solution)/shard_map/ppermute | solution.py:8
  160.1 11.3 %collective-permute-start.14 = (bf16[2,1,4,64,128]{4,3,2,1,0:T(8,128)(2,1)S(1)}, bf16[2,1,4,64,128]{4,3,2,1,0:T(8,128)(2,1)S(1)}, u32[]{:S(2)}, u32[]{:S(2)}) collective-permute-start(bf16[2,1,4,64,128]{4,3,2,1,0:T(8,128)(2,1)S(1)} %constant_dynamic-slice_fusion.45), channel_id=1, source_target_pairs={{0,8},{1,9},{2,10},{3,11},{4,12},{5,13},{6,14},{7,15},{8,0},{9,1},... | collective-permute-start | bytes 393224 | tf_op jit(solution)/shard_map/ppermute | solution.py:8
  176.6 9.0 %collective-permute-start.16 = (bf16[16,64,128]{2,1,0:T(8,128)(2,1)S(1)}, bf16[16,64,128]{2,1,0:T(8,128)(2,1)S(1)}, u32[]{:S(2)}, u32[]{:S(2)}) collective-permute-start(bf16[16,64,128]{2,1,0:T(8,128)(2,1)S(1)} %bitcast.372), channel_id=1, source_target_pairs={{0,32},{1,33},{2,34},{3,35},{4,36},{5,37},{6,38},{7,39},{8,40},{9,... | collective-permute-start | bytes 786440 | tf_op jit(solution)/shard_map/ppermute | solution.py:8
  204.1 10.4 %collective-permute-start.19 = (bf16[2,1,4,64,128]{4,3,2,1,0:T(8,128)(2,1)S(1)}, bf16[2,1,4,64,128]{4,3,2,1,0:T(8,128)(2,1)S(1)}, u32[]{:S(2)}, u32[]{:S(2)}) collective-permute-start(bf16[2,1,4,64,128]{4,3,2,1,0:T(8,128)(2,1)S(1)} %constant_dynamic-slice_fusion.41), channel_id=1, source_target_pairs={{0,8},{1,9},{2,10},{3,11},{4,12},{5,13},{6,14},{7,15},{8,0},{9,1},... | collective-permute-start | bytes 393224 | tf_op jit(solution)/shard_map/ppermute | solution.py:8
  219.6 8.3 %collective-permute-start.21 = (bf16[16,64,128]{2,1,0:T(8,128)(2,1)S(1)}, bf16[16,64,128]{2,1,0:T(8,128)(2,1)S(1)}, u32[]{:S(2)}, u32[]{:S(2)}) collective-permute-start(bf16[16,64,128]{2,1,0:T(8,128)(2,1)S(1)} %bitcast.382), channel_id=1, source_target_pairs={{0,64},{64,128},{128,192},{1,65},{65,129},{129,193},{2,66},{66,130... | collective-permute-start | bytes 786440 | tf_op jit(solution)/shard_map/ppermute | solution.py:14
  241.5 8.5 %collective-permute-start.24 = (bf16[4,1,2,64,128]{4,3,2,1,0:T(8,128)(2,1)S(1)}, bf16[4,1,2,64,128]{4,3,2,1,0:T(8,128)(2,1)S(1)}, u32[]{:S(2)}, u32[]{:S(2)}) collective-permute-start(bf16[4,1,2,64,128]{4,3,2,1,0:T(8,128)(2,1)S(1)} %constant_dynamic-slice_fusion.38), channel_id=1, source_target_pairs={{0,4},{1,5},{2,6},{3,7},{4,0},{5,1},{6,2},{7,3},{8,12},{9,13},{10,... | collective-permute-start | bytes 393224 | tf_op jit(solution)/shard_map/ppermute | solution.py:8
  250.0 11.8 %collective-permute-start.25 = (bf16[2,1,4,64,128]{4,3,2,1,0:T(8,128)(2,1)S(1)}, bf16[2,1,4,64,128]{4,3,2,1,0:T(8,128)(2,1)S(1)}, u32[]{:S(2)}, u32[]{:S(2)}) collective-permute-start(bf16[2,1,4,64,128]{4,3,2,1,0:T(8,128)(2,1)S(1)} %constant_dynamic-slice_fusion.37), channel_id=1, source_target_pairs={{0,8},{1,9},{2,10},{3,11},{4,12},{5,13},{6,14},{7,15},{8,0},{9,1},... | collective-permute-start | bytes 393224 | tf_op jit(solution)/shard_map/ppermute | solution.py:8
  267.4 9.2 %collective-permute-start.27 = (bf16[16,64,128]{2,1,0:T(8,128)(2,1)S(1)}, bf16[16,64,128]{2,1,0:T(8,128)(2,1)S(1)}, u32[]{:S(2)}, u32[]{:S(2)}) collective-permute-start(bf16[16,64,128]{2,1,0:T(8,128)(2,1)S(1)} %bitcast.391), channel_id=1, source_target_pairs={{0,32},{1,33},{2,34},{3,35},{4,36},{5,37},{6,38},{7,39},{8,40},{9,... | collective-permute-start | bytes 786440 | tf_op jit(solution)/shard_map/ppermute | solution.py:8
  294.8 10.3 %collective-permute-start.30 = (bf16[2,1,4,64,128]{4,3,2,1,0:T(8,128)(2,1)S(1)}, bf16[2,1,4,64,128]{4,3,2,1,0:T(8,128)(2,1)S(1)}, u32[]{:S(2)}, u32[]{:S(2)}) collective-permute-start(bf16[2,1,4,64,128]{4,3,2,1,0:T(8,128)(2,1)S(1)} %constant_dynamic-slice_fusion.33), channel_id=1, source_target_pairs={{0,8},{1,9},{2,10},{3,11},{4,12},{5,13},{6,14},{7,15},{8,0},{9,1},... | collective-permute-start | bytes 393224 | tf_op jit(solution)/shard_map/ppermute | solution.py:8
  332.4 8.5 %collective-permute-start.35 = (bf16[4,1,2,64,128]{4,3,2,1,0:T(8,128)(2,1)S(1)}, bf16[4,1,2,64,128]{4,3,2,1,0:T(8,128)(2,1)S(1)}, u32[]{:S(2)}, u32[]{:S(2)}) collective-permute-start(bf16[4,1,2,64,128]{4,3,2,1,0:T(8,128)(2,1)S(1)} %constant_dynamic-slice_fusion.30), channel_id=1, source_target_pairs={{0,4},{1,5},{2,6},{3,7},{4,0},{5,1},{6,2},{7,3},{8,12},{9,13},{10,... | collective-permute-start | bytes 393224 | tf_op jit(solution)/shard_map/ppermute | solution.py:8
  340.9 11.8 %collective-permute-start.36 = (bf16[2,1,4,64,128]{4,3,2,1,0:T(8,128)(2,1)S(1)}, bf16[2,1,4,64,128]{4,3,2,1,0:T(8,128)(2,1)S(1)}, u32[]{:S(2)}, u32[]{:S(2)}) collective-permute-start(bf16[2,1,4,64,128]{4,3,2,1,0:T(8,128)(2,1)S(1)} %constant_dynamic-slice_fusion.29), channel_id=1, source_target_pairs={{0,8},{1,9},{2,10},{3,11},{4,12},{5,13},{6,14},{7,15},{8,0},{9,1},... | collective-permute-start | bytes 393224 | tf_op jit(solution)/shard_map/ppermute | solution.py:8
  358.3 9.1 %collective-permute-start.38 = (bf16[16,64,128]{2,1,0:T(8,128)(2,1)S(1)}, bf16[16,64,128]{2,1,0:T(8,128)(2,1)S(1)}, u32[]{:S(2)}, u32[]{:S(2)}) collective-permute-start(bf16[16,64,128]{2,1,0:T(8,128)(2,1)S(1)} %bitcast.410), channel_id=1, source_target_pairs={{0,32},{1,33},{2,34},{3,35},{4,36},{5,37},{6,38},{7,39},{8,40},{9,... | collective-permute-start | bytes 786440 | tf_op jit(solution)/shard_map/ppermute | solution.py:8
  385.7 10.3 %collective-permute-start.41 = (bf16[2,1,4,64,128]{4,3,2,1,0:T(8,128)(2,1)S(1)}, bf16[2,1,4,64,128]{4,3,2,1,0:T(8,128)(2,1)S(1)}, u32[]{:S(2)}, u32[]{:S(2)}) collective-permute-start(bf16[2,1,4,64,128]{4,3,2,1,0:T(8,128)(2,1)S(1)} %constant_dynamic-slice_fusion.25), channel_id=1, source_target_pairs={{0,8},{1,9},{2,10},{3,11},{4,12},{5,13},{6,14},{7,15},{8,0},{9,1},... | collective-permute-start | bytes 393224 | tf_op jit(solution)/shard_map/ppermute | solution.py:8
  401.1 8.3 %collective-permute-start.43 = (bf16[16,64,128]{2,1,0:T(8,128)(2,1)S(1)}, bf16[16,64,128]{2,1,0:T(8,128)(2,1)S(1)}, u32[]{:S(2)}, u32[]{:S(2)}) collective-permute-start(bf16[16,64,128]{2,1,0:T(8,128)(2,1)S(1)} %bitcast.303), channel_id=1, source_target_pairs={{0,64},{64,128},{128,192},{1,65},{65,129},{129,193},{2,66},{66,130... | collective-permute-start | bytes 786440 | tf_op jit(solution)/shard_map/ppermute | solution.py:14
  423.1 8.5 %collective-permute-start.46 = (bf16[4,1,2,64,128]{4,3,2,1,0:T(8,128)(2,1)S(1)}, bf16[4,1,2,64,128]{4,3,2,1,0:T(8,128)(2,1)S(1)}, u32[]{:S(2)}, u32[]{:S(2)}) collective-permute-start(bf16[4,1,2,64,128]{4,3,2,1,0:T(8,128)(2,1)S(1)} %constant_dynamic-slice_fusion.22), channel_id=1, source_target_pairs={{0,4},{1,5},{2,6},{3,7},{4,0},{5,1},{6,2},{7,3},{8,12},{9,13},{10,... | collective-permute-start | bytes 393224 | tf_op jit(solution)/shard_map/ppermute | solution.py:8
  431.6 11.8 %collective-permute-start.47 = (bf16[2,1,4,64,128]{4,3,2,1,0:T(8,128)(2,1)S(1)}, bf16[2,1,4,64,128]{4,3,2,1,0:T(8,128)(2,1)S(1)}, u32[]{:S(2)}, u32[]{:S(2)}) collective-permute-start(bf16[2,1,4,64,128]{4,3,2,1,0:T(8,128)(2,1)S(1)} %constant_dynamic-slice_fusion.21), channel_id=1, source_target_pairs={{0,8},{1,9},{2,10},{3,11},{4,12},{5,13},{6,14},{7,15},{8,0},{9,1},... | collective-permute-start | bytes 393224 | tf_op jit(solution)/shard_map/ppermute | solution.py:8
  449.0 9.4 %collective-permute-start.49 = (bf16[16,64,128]{2,1,0:T(8,128)(2,1)S(1)}, bf16[16,64,128]{2,1,0:T(8,128)(2,1)S(1)}, u32[]{:S(2)}, u32[]{:S(2)}) collective-permute-start(bf16[16,64,128]{2,1,0:T(8,128)(2,1)S(1)} %bitcast.420), channel_id=1, source_target_pairs={{0,32},{1,33},{2,34},{3,35},{4,36},{5,37},{6,38},{7,39},{8,40},{9,... | collective-permute-start | bytes 786440 | tf_op jit(solution)/shard_map/ppermute | solution.py:8
  476.6 10.3 %collective-permute-start.52 = (bf16[2,1,4,64,128]{4,3,2,1,0:T(8,128)(2,1)S(1)}, bf16[2,1,4,64,128]{4,3,2,1,0:T(8,128)(2,1)S(1)}, u32[]{:S(2)}, u32[]{:S(2)}) collective-permute-start(bf16[2,1,4,64,128]{4,3,2,1,0:T(8,128)(2,1)S(1)} %constant_dynamic-slice_fusion.17), channel_id=1, source_target_pairs={{0,8},{1,9},{2,10},{3,11},{4,12},{5,13},{6,14},{7,15},{8,0},{9,1},... | collective-permute-start | bytes 393224 | tf_op jit(solution)/shard_map/ppermute | solution.py:8
  492.0 8.3 %collective-permute-start.54 = (bf16[16,64,128]{2,1,0:T(8,128)(2,1)S(1)}, bf16[16,64,128]{2,1,0:T(8,128)(2,1)S(1)}, u32[]{:S(2)}, u32[]{:S(2)}) collective-permute-start(bf16[16,64,128]{2,1,0:T(8,128)(2,1)S(1)} %bitcast.322), channel_id=1, source_target_pairs={{0,64},{64,128},{128,192},{1,65},{65,129},{129,193},{2,66},{66,130... | collective-permute-start | bytes 786440 | tf_op jit(solution)/shard_map/ppermute | solution.py:14
  514.0 8.5 %collective-permute-start.57 = (bf16[4,1,2,64,128]{4,3,2,1,0:T(8,128)(2,1)S(1)}, bf16[4,1,2,64,128]{4,3,2,1,0:T(8,128)(2,1)S(1)}, u32[]{:S(2)}, u32[]{:S(2)}) collective-permute-start(bf16[4,1,2,64,128]{4,3,2,1,0:T(8,128)(2,1)S(1)} %constant_dynamic-slice_fusion.14), channel_id=1, source_target_pairs={{0,4},{1,5},{2,6},{3,7},{4,0},{5,1},{6,2},{7,3},{8,12},{9,13},{10,... | collective-permute-start | bytes 393224 | tf_op jit(solution)/shard_map/ppermute | solution.py:8
  522.5 11.8 %collective-permute-start.58 = (bf16[2,1,4,64,128]{4,3,2,1,0:T(8,128)(2,1)S(1)}, bf16[2,1,4,64,128]{4,3,2,1,0:T(8,128)(2,1)S(1)}, u32[]{:S(2)}, u32[]{:S(2)}) collective-permute-start(bf16[2,1,4,64,128]{4,3,2,1,0:T(8,128)(2,1)S(1)} %constant_dynamic-slice_fusion.13), channel_id=1, source_target_pairs={{0,8},{1,9},{2,10},{3,11},{4,12},{5,13},{6,14},{7,15},{8,0},{9,1},... | collective-permute-start | bytes 393224 | tf_op jit(solution)/shard_map/ppermute | solution.py:8
  539.9 9.2 %collective-permute-start.60 = (bf16[16,64,128]{2,1,0:T(8,128)(2,1)S(1)}, bf16[16,64,128]{2,1,0:T(8,128)(2,1)S(1)}, u32[]{:S(2)}, u32[]{:S(2)}) collective-permute-start(bf16[16,64,128]{2,1,0:T(8,128)(2,1)S(1)} %bitcast.430), channel_id=1, source_target_pairs={{0,32},{1,33},{2,34},{3,35},{4,36},{5,37},{6,38},{7,39},{8,40},{9,... | collective-permute-start | bytes 786440 | tf_op jit(solution)/shard_map/ppermute | solution.py:8
  567.3 10.3 %collective-permute-start.63 = (bf16[2,1,4,64,128]{4,3,2,1,0:T(8,128)(2,1)S(1)}, bf16[2,1,4,64,128]{4,3,2,1,0:T(8,128)(2,1)S(1)}, u32[]{:S(2)}, u32[]{:S(2)}) collective-permute-start(bf16[2,1,4,64,128]{4,3,2,1,0:T(8,128)(2,1)S(1)} %constant_dynamic-slice_fusion.9), channel_id=1, source_target_pairs={{0,8},{1,9},{2,10},{3,11},{4,12},{5,13},{6,14},{7,15},{8,0},{9,1},... | collective-permute-start | bytes 393224 | tf_op jit(solution)/shard_map/ppermute | solution.py:8
  604.9 8.5 %collective-permute-start.68 = (bf16[4,1,2,64,128]{4,3,2,1,0:T(8,128)(2,1)S(1)}, bf16[4,1,2,64,128]{4,3,2,1,0:T(8,128)(2,1)S(1)}, u32[]{:S(2)}, u32[]{:S(2)}) collective-permute-start(bf16[4,1,2,64,128]{4,3,2,1,0:T(8,128)(2,1)S(1)} %constant_dynamic-slice_fusion.6), channel_id=1, source_target_pairs={{0,4},{1,5},{2,6},{3,7},{4,0},{5,1},{6,2},{7,3},{8,12},{9,13},{10,... | collective-permute-start | bytes 393224 | tf_op jit(solution)/shard_map/ppermute | solution.py:8
  613.4 11.8 %collective-permute-start.69 = (bf16[2,1,4,64,128]{4,3,2,1,0:T(8,128)(2,1)S(1)}, bf16[2,1,4,64,128]{4,3,2,1,0:T(8,128)(2,1)S(1)}, u32[]{:S(2)}, u32[]{:S(2)}) collective-permute-start(bf16[2,1,4,64,128]{4,3,2,1,0:T(8,128)(2,1)S(1)} %constant_dynamic-slice_fusion.5), channel_id=1, source_target_pairs={{0,8},{1,9},{2,10},{3,11},{4,12},{5,13},{6,14},{7,15},{8,0},{9,1},... | collective-permute-start | bytes 393224 | tf_op jit(solution)/shard_map/ppermute | solution.py:8
  630.8 9.1 %collective-permute-start.71 = (bf16[16,64,128]{2,1,0:T(8,128)(2,1)S(1)}, bf16[16,64,128]{2,1,0:T(8,128)(2,1)S(1)}, u32[]{:S(2)}, u32[]{:S(2)}) collective-permute-start(bf16[16,64,128]{2,1,0:T(8,128)(2,1)S(1)} %bitcast.353), channel_id=1, source_target_pairs={{0,32},{1,33},{2,34},{3,35},{4,36},{5,37},{6,38},{7,39},{8,40},{9,... | collective-permute-start | bytes 786440 | tf_op jit(solution)/shard_map/ppermute | solution.py:8
  658.2 10.3 %collective-permute-start.74 = (bf16[2,1,4,64,128]{4,3,2,1,0:T(8,128)(2,1)S(1)}, bf16[2,1,4,64,128]{4,3,2,1,0:T(8,128)(2,1)S(1)}, u32[]{:S(2)}, u32[]{:S(2)}) collective-permute-start(bf16[2,1,4,64,128]{4,3,2,1,0:T(8,128)(2,1)S(1)} %constant_dynamic-slice_fusion.1), channel_id=1, source_target_pairs={{0,8},{1,9},{2,10},{3,11},{4,12},{5,13},{6,14},{7,15},{8,0},{9,1},... | collective-permute-start | bytes 393224 | tf_op jit(solution)/shard_map/ppermute | solution.py:8
  (51 other events, 498.6 us)
where the time goes:
time: 700 us; the launch traced here: 690 us
  waiting for transfers between devices  428 us (61%)
  matrix products  114 us (16%)
  starting transfers between devices  94.7 us (14%)
  local copies, waits for them, and re-layouts  35 us (5%)
  blocking collectives  15.9 us (2%)
    ppermute x70, waiting for transfers between devices, from_partner(): lax.ppermute(array, axis, [(i, i ^ 1 << stride) for i in range(lax.axis_s...  405 us
    dot_general x14, matrix products, apply_layer(): summed = jnp.dot(matrix, flat_group, preferred_element_type=jnp.float32)  96 us
    ppermute x70, starting transfers between devices, from_partner(): lax.ppermute(array, axis, [(i, i ^ 1 << stride) for i in range(lax.axis_s...  69.2 us
    another operation x2, local copies, waits for them, and re-layouts, permuted_weights(): weights.reshape(blocks, tile_size, fan_count, row_width // fan_count)  25.7 us
    ppermute x6, starting transfers between devices, passed_along(): lax.ppermute(value, axis, [(source, source + steps) for source in range(i...  25.5 us
    ppermute x6, waiting for transfers between devices, passed_along(): lax.ppermute(value, axis, [(source, source + steps) for source in range(i...  23.1 us
    dot_general x2, matrix products, permuted_weights(): jnp.einsum('jakc,jkm->jamc', shaped, onehot, preferred_element_type=jnp.f...  18.1 us
    all_to_all x1, blocking collectives, body(): lax.all_to_all(results[:, None], 'segment', split_axis=0, concat_axis=1,...  15.9 us
  transfers between devices with their start and end apart: 76, of which 73 were waited for; matrix products, arithmetic and copies ran while one was open for 7% of the time, Pallas kernels for 0%

commit v1 on v0

--- a/solution.py
+++ b/solution.py
@@ -1,7 +1,23 @@
+import functools
 import jax
 import jax.numpy as jnp
 from jax import lax
 from jax.sharding import PartitionSpec as P
+
+
+def match_islands(unit, along_axis):
+    return jnp.concatenate(
+        lax.all_to_all(
+            jnp.stack(jnp.split(unit, lax.axis_size(along_axis), axis=0)),
+            axis_name=along_axis,
+            split_axis=0,
+            concat_axis=0,
+        ),
+        axis=1,
+    )
+
+
+bind_the_cubes = functools.partial(match_islands, along_axis="segment")
 
 
 def from_partner(array, axis, stride):
@@ -83,7 +99,7 @@
             results = results.at[finished].set(present)
         if step_index + 1 < step_count:
             arriving = passed_along(present, "segment", 1)
-    gathered = lax.all_to_all(results[:, None], "segment", split_axis=0, concat_axis=1, tiled=True)
+    gathered = bind_the_cubes(results[:, None])
     return gathered[:, segments - 1]
 
 

time: 700 us -> 700 us (level)
  no operation moved by 1% of the time
where the time goes in v1:
time: 700 us; the launch traced here: 691 us
  waiting for transfers between devices  428 us (61%)
  matrix products  114 us (16%)
  starting transfers between devices  94.7 us (14%)
  local copies, waits for them, and re-layouts  34.7 us (5%)
  blocking collectives  15.9 us (2%)
    ppermute x70, waiting for transfers between devices, from_partner(): lax.ppermute(array, axis, [(i, i ^ 1 << stride) for i in range(lax.axis_s...  405 us
    dot_general x14, matrix products, apply_layer(): summed = jnp.dot(matrix, flat_group, preferred_element_type=jnp.float32)  96 us
    ppermute x70, starting transfers between devices, from_partner(): lax.ppermute(array, axis, [(i, i ^ 1 << stride) for i in range(lax.axis_s...  69.2 us
    another operation x2, local copies, waits for them, and re-layouts, permuted_weights(): weights.reshape(blocks, tile_size, fan_count, row_width // fan_count)  25.7 us
    ppermute x6, starting transfers between devices, passed_along(): lax.ppermute(value, axis, [(source, source + steps) for source in range(i...  25.5 us
    ppermute x6, waiting for transfers between devices, passed_along(): lax.ppermute(value, axis, [(source, source + steps) for source in range(i...  23.1 us
    dot_general x2, matrix products, permuted_weights(): jnp.einsum('jakc,jkm->jamc', shaped, onehot, preferred_element_type=jnp.f...  18.1 us
    all_to_all x1, blocking collectives, match_islands(): lax.all_to_all(jnp.stack(jnp.split(unit, lax.axis_size(along_axis), axis=...  15.9 us
  transfers between devices with their start and end apart: 76, of which 73 were waited for; matrix products, arithmetic and copies ran while one was open for 7% of the time, Pallas kernels for 0%

profile of v1, /device:TPU:96, one launch (start us, length us, event | category | flops | bytes accessed | tf_op | source)
XLA Modules:
  0.0 690.6 jit_solution(12734978153139314345)
XLA Ops:
  7.4 12.9 %reshape_squeeze.7 = bf16[16,64,32,64]{3,2,1,0:T(8,128)(2,1)} reshape(bf16[1,16,64,2048]{3,2,1,0:T(8,128)(2,1)} %get-tuple-element.53) | data formatting | bytes 8388608 | tf_op jit(solution)/shard_map/reshape;squeeze | solution.py:36
  20.3 9.1 %convert_bitcast_fusion = bf16[16,64,32,64]{3,2,1,0:T(8,128)(2,1)} fusion(bf16[16,64,32,64]{3,2,1,0:T(8,128)(2,1)} %reshape_squeeze.7, s32[16,32]{1,0:T(8,128)S(1)} %get-tuple-element.57), kind=kOutput, calls=%fused_computation | convolution fusion | flops 136331264 | bytes 8390656 | tf_op jit(solution)/shard_map/jakc,jkm->jamc/dot_general | solution.py:40
  29.3 9.2 %fusion.163 = bf16[16,64,128]{2,1,0:T(8,128)(2,1)S(1)} fusion(bf16[16,64,32,64]{3,2,1,0:T(8,128)(2,1)} %convert_bitcast_fusion, bf16[16,64,128]{2,1,0:T(8,128)(2,1)S(1)} %collective-permute-done, bf16[16,64,128]{2,1,0:T(8,128)(2,1)S(1)} %select_bitcast_fusion, pred[]{:T(512)S(6)} %eq.137, f32[16,64]{1,0:T(8,128)S(1)} %get-tuple-element.56), kind=kOutput, calls=%fused_computation.75 | convolution fusion | flops 538050560 | bytes 4984833 | tf_op jit(solution)/shard_map/dot_general | solution.py:56
  44.7 8.6 %collective-permute-done.2 = bf16[4,1,2,64,128]{4,3,2,1,0:T(8,128)(2,1)S(1)} collective-permute-done((bf16[4,1,2,64,128]{4,3,2,1,0:T(8,128)(2,1)S(1)}, bf16[4,1,2,64,128]{4,3,2,1,0:T(8,128)(2,1)S(1)}, u32[]{:S(2)}, u32[]{:S(2)}) %collective-permute-start.2) | collective-permute-done | bytes 131104 | tf_op jit(solution)/shard_map/ppermute | solution.py:24
  58.2 7.5 %collective-permute-done.3 = bf16[2,1,4,64,128]{4,3,2,1,0:T(8,128)(2,1)S(1)} collective-permute-done((bf16[2,1,4,64,128]{4,3,2,1,0:T(8,128)(2,1)S(1)}, bf16[2,1,4,64,128]{4,3,2,1,0:T(8,128)(2,1)S(1)}, u32[]{:S(2)}, u32[]{:S(2)}) %collective-permute-start.3) | collective-permute-done | bytes 131104 | tf_op jit(solution)/shard_map/ppermute | solution.py:24
  67.4 12.9 %reshape_squeeze.6 = bf16[16,64,32,64]{3,2,1,0:T(8,128)(2,1)} reshape(bf16[1,16,64,2048]{3,2,1,0:T(8,128)(2,1)} %get-tuple-element.54) | data formatting | bytes 8388608 | tf_op jit(solution)/shard_map/reshape;squeeze | solution.py:36
  83.1 9.0 %convert_bitcast_fusion.1 = bf16[16,64,32,64]{3,2,1,0:T(8,128)(2,1)} fusion(bf16[16,64,32,64]{3,2,1,0:T(8,128)(2,1)} %reshape_squeeze.6, s32[16,32]{1,0:T(8,128)S(1)} %get-tuple-element.58), kind=kOutput, calls=%fused_computation.1 | convolution fusion | flops 136331264 | bytes 8390656 | tf_op jit(solution)/shard_map/jakc,jkm->jamc/dot_general | solution.py:40
  92.1 9.2 %fusion.184 = bf16[16,64,128]{2,1,0:T(8,128)(2,1)S(1)} fusion(bf16[16,64,32,64]{3,2,1,0:T(8,128)(2,1)} %convert_bitcast_fusion.1, bf16[16,64,128]{2,1,0:T(8,128)(2,1)S(1)} %collective-permute-done.5, bf16[16,64,128]{2,1,0:T(8,128)(2,1)S(1)} %bitcast.336, pred[]{:T(512)S(6)} %eq.132, f32[16,64]{1,0:T(8,128)S(1)} %get-tuple-element.55), kind=kOutput, calls=%fused_computation.82 | convolution fusion | flops 538050560 | bytes 4984833 | tf_op jit(solution)/shard_map/dot_general | solution.py:56
  137.5 10.0 %fusion.160 = bf16[16,64,128]{2,1,0:T(8,128)(2,1)S(1)} fusion(bf16[16,64,32,64]{3,2,1,0:T(8,128)(2,1)} %convert_bitcast_fusion, bf16[16,64,128]{2,1,0:T(8,128)(2,1)S(1)} %collective-permute-done.11, bf16[16,64,128]{2,1,0:T(8,128)(2,1)S(1)} %bitcast_select_fusion, pred[]{:T(512)S(6)} %eq.137, f32[16,64]{1,0:T(8,128)S(1)} %get-tuple-element.56), kind=kOutput, calls=%fused_computation.74 | convolution fusion | flops 538050560 | bytes 4984833 | tf_op jit(solution)/shard_map/dot_general | solution.py:56
  163.5 7.9 %collective-permute-done.14 = bf16[2,1,4,64,128]{4,3,2,1,0:T(8,128)(2,1)S(1)} collective-permute-done((bf16[2,1,4,64,128]{4,3,2,1,0:T(8,128)(2,1)S(1)}, bf16[2,1,4,64,128]{4,3,2,1,0:T(8,128)(2,1)S(1)}, u32[]{:S(2)}, u32[]{:S(2)}) %collective-permute-start.14) | collective-permute-done | bytes 131104 | tf_op jit(solution)/shard_map/ppermute | solution.py:24
  177.9 7.8 %collective-permute-done.16 = bf16[16,64,128]{2,1,0:T(8,128)(2,1)S(1)} collective-permute-done((bf16[16,64,128]{2,1,0:T(8,128)(2,1)S(1)}, bf16[16,64,128]{2,1,0:T(8,128)(2,1)S(1)}, u32[]{:S(2)}, u32[]{:S(2)}) %collective-permute-start.16) | collective-permute-done | bytes 262176 | tf_op jit(solution)/shard_map/ppermute | solution.py:24
  241.6 8.4 %collective-permute-done.24 = bf16[4,1,2,64,128]{4,3,2,1,0:T(8,128)(2,1)S(1)} collective-permute-done((bf16[4,1,2,64,128]{4,3,2,1,0:T(8,128)(2,1)S(1)}, bf16[4,1,2,64,128]{4,3,2,1,0:T(8,128)(2,1)S(1)}, u32[]{:S(2)}, u32[]{:S(2)}) %collective-permute-start.24) | collective-permute-done | bytes 131104 | tf_op jit(solution)/shard_map/ppermute | solution.py:24
  253.1 8.8 %collective-permute-done.25 = bf16[2,1,4,64,128]{4,3,2,1,0:T(8,128)(2,1)S(1)} collective-permute-done((bf16[2,1,4,64,128]{4,3,2,1,0:T(8,128)(2,1)S(1)}, bf16[2,1,4,64,128]{4,3,2,1,0:T(8,128)(2,1)S(1)}, u32[]{:S(2)}, u32[]{:S(2)}) %collective-permute-start.25) | collective-permute-done | bytes 131104 | tf_op jit(solution)/shard_map/ppermute | solution.py:24
  268.5 8.1 %collective-permute-done.27 = bf16[16,64,128]{2,1,0:T(8,128)(2,1)S(1)} collective-permute-done((bf16[16,64,128]{2,1,0:T(8,128)(2,1)S(1)}, bf16[16,64,128]{2,1,0:T(8,128)(2,1)S(1)}, u32[]{:S(2)}, u32[]{:S(2)}) %collective-permute-start.27) | collective-permute-done | bytes 262176 | tf_op jit(solution)/shard_map/ppermute | solution.py:24
  297.9 7.3 %collective-permute-done.30 = bf16[2,1,4,64,128]{4,3,2,1,0:T(8,128)(2,1)S(1)} collective-permute-done((bf16[2,1,4,64,128]{4,3,2,1,0:T(8,128)(2,1)S(1)}, bf16[2,1,4,64,128]{4,3,2,1,0:T(8,128)(2,1)S(1)}, u32[]{:S(2)}, u32[]{:S(2)}) %collective-permute-start.30) | collective-permute-done | bytes 131104 | tf_op jit(solution)/shard_map/ppermute | solution.py:24
  332.5 8.4 %collective-permute-done.35 = bf16[4,1,2,64,128]{4,3,2,1,0:T(8,128)(2,1)S(1)} collective-permute-done((bf16[4,1,2,64,128]{4,3,2,1,0:T(8,128)(2,1)S(1)}, bf16[4,1,2,64,128]{4,3,2,1,0:T(8,128)(2,1)S(1)}, u32[]{:S(2)}, u32[]{:S(2)}) %collective-permute-start.35) | collective-permute-done | bytes 131104 | tf_op jit(solution)/shard_map/ppermute | solution.py:24
  344.0 8.8 %collective-permute-done.36 = bf16[2,1,4,64,128]{4,3,2,1,0:T(8,128)(2,1)S(1)} collective-permute-done((bf16[2,1,4,64,128]{4,3,2,1,0:T(8,128)(2,1)S(1)}, bf16[2,1,4,64,128]{4,3,2,1,0:T(8,128)(2,1)S(1)}, u32[]{:S(2)}, u32[]{:S(2)}) %collective-permute-start.36) | collective-permute-done | bytes 131104 | tf_op jit(solution)/shard_map/ppermute | solution.py:24
  359.4 8.1 %collective-permute-done.38 = bf16[16,64,128]{2,1,0:T(8,128)(2,1)S(1)} collective-permute-done((bf16[16,64,128]{2,1,0:T(8,128)(2,1)S(1)}, bf16[16,64,128]{2,1,0:T(8,128)(2,1)S(1)}, u32[]{:S(2)}, u32[]{:S(2)}) %collective-permute-start.38) | collective-permute-done | bytes 262176 | tf_op jit(solution)/shard_map/ppermute | solution.py:24
  388.7 7.3 %collective-permute-done.41 = bf16[2,1,4,64,128]{4,3,2,1,0:T(8,128)(2,1)S(1)} collective-permute-done((bf16[2,1,4,64,128]{4,3,2,1,0:T(8,128)(2,1)S(1)}, bf16[2,1,4,64,128]{4,3,2,1,0:T(8,128)(2,1)S(1)}, u32[]{:S(2)}, u32[]{:S(2)}) %collective-permute-start.41) | collective-permute-done | bytes 131104 | tf_op jit(solution)/shard_map/ppermute | solution.py:24
  423.2 8.4 %collective-permute-done.46 = bf16[4,1,2,64,128]{4,3,2,1,0:T(8,128)(2,1)S(1)} collective-permute-done((bf16[4,1,2,64,128]{4,3,2,1,0:T(8,128)(2,1)S(1)}, bf16[4,1,2,64,128]{4,3,2,1,0:T(8,128)(2,1)S(1)}, u32[]{:S(2)}, u32[]{:S(2)}) %collective-permute-start.46) | collective-permute-done | bytes 131104 | tf_op jit(solution)/shard_map/ppermute | solution.py:24
  434.7 8.8 %collective-permute-done.47 = bf16[2,1,4,64,128]{4,3,2,1,0:T(8,128)(2,1)S(1)} collective-permute-done((bf16[2,1,4,64,128]{4,3,2,1,0:T(8,128)(2,1)S(1)}, bf16[2,1,4,64,128]{4,3,2,1,0:T(8,128)(2,1)S(1)}, u32[]{:S(2)}, u32[]{:S(2)}) %collective-permute-start.47) | collective-permute-done | bytes 131104 | tf_op jit(solution)/shard_map/ppermute | solution.py:24
  450.3 8.1 %collective-permute-done.49 = bf16[16,64,128]{2,1,0:T(8,128)(2,1)S(1)} collective-permute-done((bf16[16,64,128]{2,1,0:T(8,128)(2,1)S(1)}, bf16[16,64,128]{2,1,0:T(8,128)(2,1)S(1)}, u32[]{:S(2)}, u32[]{:S(2)}) %collective-permute-start.49) | collective-permute-done | bytes 262176 | tf_op jit(solution)/shard_map/ppermute | solution.py:24
  479.6 7.3 %collective-permute-done.52 = bf16[2,1,4,64,128]{4,3,2,1,0:T(8,128)(2,1)S(1)} collective-permute-done((bf16[2,1,4,64,128]{4,3,2,1,0:T(8,128)(2,1)S(1)}, bf16[2,1,4,64,128]{4,3,2,1,0:T(8,128)(2,1)S(1)}, u32[]{:S(2)}, u32[]{:S(2)}) %collective-permute-start.52) | collective-permute-done | bytes 131104 | tf_op jit(solution)/shard_map/ppermute | solution.py:24
  514.1 8.4 %collective-permute-done.57 = bf16[4,1,2,64,128]{4,3,2,1,0:T(8,128)(2,1)S(1)} collective-permute-done((bf16[4,1,2,64,128]{4,3,2,1,0:T(8,128)(2,1)S(1)}, bf16[4,1,2,64,128]{4,3,2,1,0:T(8,128)(2,1)S(1)}, u32[]{:S(2)}, u32[]{:S(2)}) %collective-permute-start.57) | collective-permute-done | bytes 131104 | tf_op jit(solution)/shard_map/ppermute | solution.py:24
  525.6 8.8 %collective-permute-done.58 = bf16[2,1,4,64,128]{4,3,2,1,0:T(8,128)(2,1)S(1)} collective-permute-done((bf16[2,1,4,64,128]{4,3,2,1,0:T(8,128)(2,1)S(1)}, bf16[2,1,4,64,128]{4,3,2,1,0:T(8,128)(2,1)S(1)}, u32[]{:S(2)}, u32[]{:S(2)}) %collective-permute-start.58) | collective-permute-done | bytes 131104 | tf_op jit(solution)/shard_map/ppermute | solution.py:24
  541.0 8.1 %collective-permute-done.60 = bf16[16,64,128]{2,1,0:T(8,128)(2,1)S(1)} collective-permute-done((bf16[16,64,128]{2,1,0:T(8,128)(2,1)S(1)}, bf16[16,64,128]{2,1,0:T(8,128)(2,1)S(1)}, u32[]{:S(2)}, u32[]{:S(2)}) %collective-permute-start.60) | collective-permute-done | bytes 262176 | tf_op jit(solution)/shard_map/ppermute | solution.py:24
  570.3 7.3 %collective-permute-done.63 = bf16[2,1,4,64,128]{4,3,2,1,0:T(8,128)(2,1)S(1)} collective-permute-done((bf16[2,1,4,64,128]{4,3,2,1,0:T(8,128)(2,1)S(1)}, bf16[2,1,4,64,128]{4,3,2,1,0:T(8,128)(2,1)S(1)}, u32[]{:S(2)}, u32[]{:S(2)}) %collective-permute-start.63) | collective-permute-done | bytes 131104 | tf_op jit(solution)/shard_map/ppermute | solution.py:24
  605.0 8.4 %collective-permute-done.68 = bf16[4,1,2,64,128]{4,3,2,1,0:T(8,128)(2,1)S(1)} collective-permute-done((bf16[4,1,2,64,128]{4,3,2,1,0:T(8,128)(2,1)S(1)}, bf16[4,1,2,64,128]{4,3,2,1,0:T(8,128)(2,1)S(1)}, u32[]{:S(2)}, u32[]{:S(2)}) %collective-permute-start.68) | collective-permute-done | bytes 131104 | tf_op jit(solution)/shard_map/ppermute | solution.py:24
  616.5 8.8 %collective-permute-done.69 = bf16[2,1,4,64,128]{4,3,2,1,0:T(8,128)(2,1)S(1)} collective-permute-done((bf16[2,1,4,64,128]{4,3,2,1,0:T(8,128)(2,1)S(1)}, bf16[2,1,4,64,128]{4,3,2,1,0:T(8,128)(2,1)S(1)}, u32[]{:S(2)}, u32[]{:S(2)}) %collective-permute-start.69) | collective-permute-done | bytes 131104 | tf_op jit(solution)/shard_map/ppermute | solution.py:24
  631.8 8.1 %collective-permute-done.71 = bf16[16,64,128]{2,1,0:T(8,128)(2,1)S(1)} collective-permute-done((bf16[16,64,128]{2,1,0:T(8,128)(2,1)S(1)}, bf16[16,64,128]{2,1,0:T(8,128)(2,1)S(1)}, u32[]{:S(2)}, u32[]{:S(2)}) %collective-permute-start.71) | collective-permute-done | bytes 262176 | tf_op jit(solution)/shard_map/ppermute | solution.py:24
  661.2 7.3 %collective-permute-done.74 = bf16[2,1,4,64,128]{4,3,2,1,0:T(8,128)(2,1)S(1)} collective-permute-done((bf16[2,1,4,64,128]{4,3,2,1,0:T(8,128)(2,1)S(1)}, bf16[2,1,4,64,128]{4,3,2,1,0:T(8,128)(2,1)S(1)}, u32[]{:S(2)}, u32[]{:S(2)}) %collective-permute-start.74) | collective-permute-done | bytes 131104 | tf_op jit(solution)/shard_map/ppermute | solution.py:24
  673.7 15.9 %all_to_all.5 = bf16[4,1,1,16,64,128]{5,4,3,2,1,0:T(8,128)(2,1)S(1)} all-to-all(bf16[4,1,1,16,64,128]{5,4,3,2,1,0:T(8,128)(2,1)S(1)} %pad_maximum_fusion), channel_id=1, replica_groups=mesh['segment'=4,'blk'=64] {'segment'}, dimensions={0} | all-to-all | bytes 2097152 | tf_op jit(solution)/shard_map/all_to_all | solution.py:10
  (279 shorter events, 406.9 us)
Async XLA Ops:
  1.0 28.4 %collective-permute-start = (bf16[16,64,128]{2,1,0:T(8,128)(2,1)S(1)}, bf16[16,64,128]{2,1,0:T(8,128)(2,1)S(1)}, u32[]{:S(2)}, u32[]{:S(2)}) collective-permute-start(bf16[16,64,128]{2,1,0:T(8,128)(2,1)S(1)} %select_bitcast_fusion), channel_id=1, source_target_pairs={{0,1},{1,0},{2,3},{3,2},{4,5},{5,4},{6,7},{7,6},{8,9},{9,8},{10,11... | collective-permute-start | bytes 786440 | tf_op jit(solution)/shard_map/ppermute | solution.py:24
  44.6 8.7 %collective-permute-start.2 = (bf16[4,1,2,64,128]{4,3,2,1,0:T(8,128)(2,1)S(1)}, bf16[4,1,2,64,128]{4,3,2,1,0:T(8,128)(2,1)S(1)}, u32[]{:S(2)}, u32[]{:S(2)}) collective-permute-start(bf16[4,1,2,64,128]{4,3,2,1,0:T(8,128)(2,1)S(1)} %constant_dynamic-slice_fusion.54), channel_id=1, source_target_pairs={{0,4},{1,5},{2,6},{3,7},{4,0},{5,1},{6,2},{7,3},{8,12},{9,13},{10,... | collective-permute-start | bytes 393224 | tf_op jit(solution)/shard_map/ppermute | solution.py:24
  53.4 12.4 %collective-permute-start.3 = (bf16[2,1,4,64,128]{4,3,2,1,0:T(8,128)(2,1)S(1)}, bf16[2,1,4,64,128]{4,3,2,1,0:T(8,128)(2,1)S(1)}, u32[]{:S(2)}, u32[]{:S(2)}) collective-permute-start(bf16[2,1,4,64,128]{4,3,2,1,0:T(8,128)(2,1)S(1)} %constant_dynamic-slice_fusion.53), channel_id=1, source_target_pairs={{0,8},{1,9},{2,10},{3,11},{4,12},{5,13},{6,14},{7,15},{8,0},{9,1},... | collective-permute-start | bytes 393224 | tf_op jit(solution)/shard_map/ppermute | solution.py:24
  65.8 14.4 %collective-permute-start.4 = (bf16[1,1,8,64,128]{4,3,2,1,0:T(8,128)(2,1)S(1)}, bf16[1,1,8,64,128]{4,3,2,1,0:T(8,128)(2,1)S(1)}, u32[]{:S(2)}, u32[]{:S(2)}) collective-permute-start(bf16[1,1,8,64,128]{4,3,2,1,0:T(8,128)(2,1)S(1)} %constant_dynamic-slice_fusion.52), channel_id=1, source_target_pairs={{0,16},{1,17},{2,18},{3,19},{4,20},{5,21},{6,22},{7,23},{8,24},{9,... | collective-permute-start | bytes 393224 | tf_op jit(solution)/shard_map/ppermute | solution.py:24
  80.2 11.9 %collective-permute-start.5 = (bf16[16,64,128]{2,1,0:T(8,128)(2,1)S(1)}, bf16[16,64,128]{2,1,0:T(8,128)(2,1)S(1)}, u32[]{:S(2)}, u32[]{:S(2)}) collective-permute-start(bf16[16,64,128]{2,1,0:T(8,128)(2,1)S(1)} %bitcast.335), channel_id=1, source_target_pairs={{0,32},{1,33},{2,34},{3,35},{4,36},{5,37},{6,38},{7,39},{8,40},{9,... | collective-permute-start | bytes 786440 | tf_op jit(solution)/shard_map/ppermute | solution.py:24
  113.5 9.8 %collective-permute-start.8 = (bf16[2,1,4,64,128]{4,3,2,1,0:T(8,128)(2,1)S(1)}, bf16[2,1,4,64,128]{4,3,2,1,0:T(8,128)(2,1)S(1)}, u32[]{:S(2)}, u32[]{:S(2)}) collective-permute-start(bf16[2,1,4,64,128]{4,3,2,1,0:T(8,128)(2,1)S(1)} %constant_dynamic-slice_fusion.49), channel_id=1, source_target_pairs={{0,8},{1,9},{2,10},{3,11},{4,12},{5,13},{6,14},{7,15},{8,0},{9,1},... | collective-permute-start | bytes 393224 | tf_op jit(solution)/shard_map/ppermute | solution.py:24
  160.1 11.3 %collective-permute-start.14 = (bf16[2,1,4,64,128]{4,3,2,1,0:T(8,128)(2,1)S(1)}, bf16[2,1,4,64,128]{4,3,2,1,0:T(8,128)(2,1)S(1)}, u32[]{:S(2)}, u32[]{:S(2)}) collective-permute-start(bf16[2,1,4,64,128]{4,3,2,1,0:T(8,128)(2,1)S(1)} %constant_dynamic-slice_fusion.45), channel_id=1, source_target_pairs={{0,8},{1,9},{2,10},{3,11},{4,12},{5,13},{6,14},{7,15},{8,0},{9,1},... | collective-permute-start | bytes 393224 | tf_op jit(solution)/shard_map/ppermute | solution.py:24
  176.6 9.0 %collective-permute-start.16 = (bf16[16,64,128]{2,1,0:T(8,128)(2,1)S(1)}, bf16[16,64,128]{2,1,0:T(8,128)(2,1)S(1)}, u32[]{:S(2)}, u32[]{:S(2)}) collective-permute-start(bf16[16,64,128]{2,1,0:T(8,128)(2,1)S(1)} %bitcast.364), channel_id=1, source_target_pairs={{0,32},{1,33},{2,34},{3,35},{4,36},{5,37},{6,38},{7,39},{8,40},{9,... | collective-permute-start | bytes 786440 | tf_op jit(solution)/shard_map/ppermute | solution.py:24
  204.1 10.4 %collective-permute-start.19 = (bf16[2,1,4,64,128]{4,3,2,1,0:T(8,128)(2,1)S(1)}, bf16[2,1,4,64,128]{4,3,2,1,0:T(8,128)(2,1)S(1)}, u32[]{:S(2)}, u32[]{:S(2)}) collective-permute-start(bf16[2,1,4,64,128]{4,3,2,1,0:T(8,128)(2,1)S(1)} %constant_dynamic-slice_fusion.41), channel_id=1, source_target_pairs={{0,8},{1,9},{2,10},{3,11},{4,12},{5,13},{6,14},{7,15},{8,0},{9,1},... | collective-permute-start | bytes 393224 | tf_op jit(solution)/shard_map/ppermute | solution.py:24
  219.6 8.3 %collective-permute-start.21 = (bf16[16,64,128]{2,1,0:T(8,128)(2,1)S(1)}, bf16[16,64,128]{2,1,0:T(8,128)(2,1)S(1)}, u32[]{:S(2)}, u32[]{:S(2)}) collective-permute-start(bf16[16,64,128]{2,1,0:T(8,128)(2,1)S(1)} %bitcast.374), channel_id=1, source_target_pairs={{0,64},{64,128},{128,192},{1,65},{65,129},{129,193},{2,66},{66,130... | collective-permute-start | bytes 786440 | tf_op jit(solution)/shard_map/ppermute | solution.py:30
  241.5 8.5 %collective-permute-start.24 = (bf16[4,1,2,64,128]{4,3,2,1,0:T(8,128)(2,1)S(1)}, bf16[4,1,2,64,128]{4,3,2,1,0:T(8,128)(2,1)S(1)}, u32[]{:S(2)}, u32[]{:S(2)}) collective-permute-start(bf16[4,1,2,64,128]{4,3,2,1,0:T(8,128)(2,1)S(1)} %constant_dynamic-slice_fusion.38), channel_id=1, source_target_pairs={{0,4},{1,5},{2,6},{3,7},{4,0},{5,1},{6,2},{7,3},{8,12},{9,13},{10,... | collective-permute-start | bytes 393224 | tf_op jit(solution)/shard_map/ppermute | solution.py:24
  250.0 11.8 %collective-permute-start.25 = (bf16[2,1,4,64,128]{4,3,2,1,0:T(8,128)(2,1)S(1)}, bf16[2,1,4,64,128]{4,3,2,1,0:T(8,128)(2,1)S(1)}, u32[]{:S(2)}, u32[]{:S(2)}) collective-permute-start(bf16[2,1,4,64,128]{4,3,2,1,0:T(8,128)(2,1)S(1)} %constant_dynamic-slice_fusion.37), channel_id=1, source_target_pairs={{0,8},{1,9},{2,10},{3,11},{4,12},{5,13},{6,14},{7,15},{8,0},{9,1},... | collective-permute-start | bytes 393224 | tf_op jit(solution)/shard_map/ppermute | solution.py:24
  267.4 9.2 %collective-permute-start.27 = (bf16[16,64,128]{2,1,0:T(8,128)(2,1)S(1)}, bf16[16,64,128]{2,1,0:T(8,128)(2,1)S(1)}, u32[]{:S(2)}, u32[]{:S(2)}) collective-permute-start(bf16[16,64,128]{2,1,0:T(8,128)(2,1)S(1)} %bitcast.383), channel_id=1, source_target_pairs={{0,32},{1,33},{2,34},{3,35},{4,36},{5,37},{6,38},{7,39},{8,40},{9,... | collective-permute-start | bytes 786440 | tf_op jit(solution)/shard_map/ppermute | solution.py:24
  294.8 10.3 %collective-permute-start.30 = (bf16[2,1,4,64,128]{4,3,2,1,0:T(8,128)(2,1)S(1)}, bf16[2,1,4,64,128]{4,3,2,1,0:T(8,128)(2,1)S(1)}, u32[]{:S(2)}, u32[]{:S(2)}) collective-permute-start(bf16[2,1,4,64,128]{4,3,2,1,0:T(8,128)(2,1)S(1)} %constant_dynamic-slice_fusion.33), channel_id=1, source_target_pairs={{0,8},{1,9},{2,10},{3,11},{4,12},{5,13},{6,14},{7,15},{8,0},{9,1},... | collective-permute-start | bytes 393224 | tf_op jit(solution)/shard_map/ppermute | solution.py:24
  332.4 8.5 %collective-permute-start.35 = (bf16[4,1,2,64,128]{4,3,2,1,0:T(8,128)(2,1)S(1)}, bf16[4,1,2,64,128]{4,3,2,1,0:T(8,128)(2,1)S(1)}, u32[]{:S(2)}, u32[]{:S(2)}) collective-permute-start(bf16[4,1,2,64,128]{4,3,2,1,0:T(8,128)(2,1)S(1)} %constant_dynamic-slice_fusion.30), channel_id=1, source_target_pairs={{0,4},{1,5},{2,6},{3,7},{4,0},{5,1},{6,2},{7,3},{8,12},{9,13},{10,... | collective-permute-start | bytes 393224 | tf_op jit(solution)/shard_map/ppermute | solution.py:24
  340.9 11.8 %collective-permute-start.36 = (bf16[2,1,4,64,128]{4,3,2,1,0:T(8,128)(2,1)S(1)}, bf16[2,1,4,64,128]{4,3,2,1,0:T(8,128)(2,1)S(1)}, u32[]{:S(2)}, u32[]{:S(2)}) collective-permute-start(bf16[2,1,4,64,128]{4,3,2,1,0:T(8,128)(2,1)S(1)} %constant_dynamic-slice_fusion.29), channel_id=1, source_target_pairs={{0,8},{1,9},{2,10},{3,11},{4,12},{5,13},{6,14},{7,15},{8,0},{9,1},... | collective-permute-start | bytes 393224 | tf_op jit(solution)/shard_map/ppermute | solution.py:24
  358.3 9.1 %collective-permute-start.38 = (bf16[16,64,128]{2,1,0:T(8,128)(2,1)S(1)}, bf16[16,64,128]{2,1,0:T(8,128)(2,1)S(1)}, u32[]{:S(2)}, u32[]{:S(2)}) collective-permute-start(bf16[16,64,128]{2,1,0:T(8,128)(2,1)S(1)} %bitcast.402), channel_id=1, source_target_pairs={{0,32},{1,33},{2,34},{3,35},{4,36},{5,37},{6,38},{7,39},{8,40},{9,... | collective-permute-start | bytes 786440 | tf_op jit(solution)/shard_map/ppermute | solution.py:24
  385.7 10.3 %collective-permute-start.41 = (bf16[2,1,4,64,128]{4,3,2,1,0:T(8,128)(2,1)S(1)}, bf16[2,1,4,64,128]{4,3,2,1,0:T(8,128)(2,1)S(1)}, u32[]{:S(2)}, u32[]{:S(2)}) collective-permute-start(bf16[2,1,4,64,128]{4,3,2,1,0:T(8,128)(2,1)S(1)} %constant_dynamic-slice_fusion.25), channel_id=1, source_target_pairs={{0,8},{1,9},{2,10},{3,11},{4,12},{5,13},{6,14},{7,15},{8,0},{9,1},... | collective-permute-start | bytes 393224 | tf_op jit(solution)/shard_map/ppermute | solution.py:24
  401.1 8.3 %collective-permute-start.43 = (bf16[16,64,128]{2,1,0:T(8,128)(2,1)S(1)}, bf16[16,64,128]{2,1,0:T(8,128)(2,1)S(1)}, u32[]{:S(2)}, u32[]{:S(2)}) collective-permute-start(bf16[16,64,128]{2,1,0:T(8,128)(2,1)S(1)} %bitcast.304), channel_id=1, source_target_pairs={{0,64},{64,128},{128,192},{1,65},{65,129},{129,193},{2,66},{66,130... | collective-permute-start | bytes 786440 | tf_op jit(solution)/shard_map/ppermute | solution.py:30
  423.1 8.5 %collective-permute-start.46 = (bf16[4,1,2,64,128]{4,3,2,1,0:T(8,128)(2,1)S(1)}, bf16[4,1,2,64,128]{4,3,2,1,0:T(8,128)(2,1)S(1)}, u32[]{:S(2)}, u32[]{:S(2)}) collective-permute-start(bf16[4,1,2,64,128]{4,3,2,1,0:T(8,128)(2,1)S(1)} %constant_dynamic-slice_fusion.22), channel_id=1, source_target_pairs={{0,4},{1,5},{2,6},{3,7},{4,0},{5,1},{6,2},{7,3},{8,12},{9,13},{10,... | collective-permute-start | bytes 393224 | tf_op jit(solution)/shard_map/ppermute | solution.py:24
  431.6 11.8 %collective-permute-start.47 = (bf16[2,1,4,64,128]{4,3,2,1,0:T(8,128)(2,1)S(1)}, bf16[2,1,4,64,128]{4,3,2,1,0:T(8,128)(2,1)S(1)}, u32[]{:S(2)}, u32[]{:S(2)}) collective-permute-start(bf16[2,1,4,64,128]{4,3,2,1,0:T(8,128)(2,1)S(1)} %constant_dynamic-slice_fusion.21), channel_id=1, source_target_pairs={{0,8},{1,9},{2,10},{3,11},{4,12},{5,13},{6,14},{7,15},{8,0},{9,1},... | collective-permute-start | bytes 393224 | tf_op jit(solution)/shard_map/ppermute | solution.py:24
  449.0 9.4 %collective-permute-start.49 = (bf16[16,64,128]{2,1,0:T(8,128)(2,1)S(1)}, bf16[16,64,128]{2,1,0:T(8,128)(2,1)S(1)}, u32[]{:S(2)}, u32[]{:S(2)}) collective-permute-start(bf16[16,64,128]{2,1,0:T(8,128)(2,1)S(1)} %bitcast.412), channel_id=1, source_target_pairs={{0,32},{1,33},{2,34},{3,35},{4,36},{5,37},{6,38},{7,39},{8,40},{9,... | collective-permute-start | bytes 786440 | tf_op jit(solution)/shard_map/ppermute | solution.py:24
  476.6 10.3 %collective-permute-start.52 = (bf16[2,1,4,64,128]{4,3,2,1,0:T(8,128)(2,1)S(1)}, bf16[2,1,4,64,128]{4,3,2,1,0:T(8,128)(2,1)S(1)}, u32[]{:S(2)}, u32[]{:S(2)}) collective-permute-start(bf16[2,1,4,64,128]{4,3,2,1,0:T(8,128)(2,1)S(1)} %constant_dynamic-slice_fusion.17), channel_id=1, source_target_pairs={{0,8},{1,9},{2,10},{3,11},{4,12},{5,13},{6,14},{7,15},{8,0},{9,1},... | collective-permute-start | bytes 393224 | tf_op jit(solution)/shard_map/ppermute | solution.py:24
  492.0 8.3 %collective-permute-start.54 = (bf16[16,64,128]{2,1,0:T(8,128)(2,1)S(1)}, bf16[16,64,128]{2,1,0:T(8,128)(2,1)S(1)}, u32[]{:S(2)}, u32[]{:S(2)}) collective-permute-start(bf16[16,64,128]{2,1,0:T(8,128)(2,1)S(1)} %bitcast.314), channel_id=1, source_target_pairs={{0,64},{64,128},{128,192},{1,65},{65,129},{129,193},{2,66},{66,130... | collective-permute-start | bytes 786440 | tf_op jit(solution)/shard_map/ppermute | solution.py:30
  514.0 8.5 %collective-permute-start.57 = (bf16[4,1,2,64,128]{4,3,2,1,0:T(8,128)(2,1)S(1)}, bf16[4,1,2,64,128]{4,3,2,1,0:T(8,128)(2,1)S(1)}, u32[]{:S(2)}, u32[]{:S(2)}) collective-permute-start(bf16[4,1,2,64,128]{4,3,2,1,0:T(8,128)(2,1)S(1)} %constant_dynamic-slice_fusion.14), channel_id=1, source_target_pairs={{0,4},{1,5},{2,6},{3,7},{4,0},{5,1},{6,2},{7,3},{8,12},{9,13},{10,... | collective-permute-start | bytes 393224 | tf_op jit(solution)/shard_map/ppermute | solution.py:24
  522.5 11.8 %collective-permute-start.58 = (bf16[2,1,4,64,128]{4,3,2,1,0:T(8,128)(2,1)S(1)}, bf16[2,1,4,64,128]{4,3,2,1,0:T(8,128)(2,1)S(1)}, u32[]{:S(2)}, u32[]{:S(2)}) collective-permute-start(bf16[2,1,4,64,128]{4,3,2,1,0:T(8,128)(2,1)S(1)} %constant_dynamic-slice_fusion.13), channel_id=1, source_target_pairs={{0,8},{1,9},{2,10},{3,11},{4,12},{5,13},{6,14},{7,15},{8,0},{9,1},... | collective-permute-start | bytes 393224 | tf_op jit(solution)/shard_map/ppermute | solution.py:24
  539.9 9.2 %collective-permute-start.60 = (bf16[16,64,128]{2,1,0:T(8,128)(2,1)S(1)}, bf16[16,64,128]{2,1,0:T(8,128)(2,1)S(1)}, u32[]{:S(2)}, u32[]{:S(2)}) collective-permute-start(bf16[16,64,128]{2,1,0:T(8,128)(2,1)S(1)} %bitcast.422), channel_id=1, source_target_pairs={{0,32},{1,33},{2,34},{3,35},{4,36},{5,37},{6,38},{7,39},{8,40},{9,... | collective-permute-start | bytes 786440 | tf_op jit(solution)/shard_map/ppermute | solution.py:24
  567.3 10.3 %collective-permute-start.63 = (bf16[2,1,4,64,128]{4,3,2,1,0:T(8,128)(2,1)S(1)}, bf16[2,1,4,64,128]{4,3,2,1,0:T(8,128)(2,1)S(1)}, u32[]{:S(2)}, u32[]{:S(2)}) collective-permute-start(bf16[2,1,4,64,128]{4,3,2,1,0:T(8,128)(2,1)S(1)} %constant_dynamic-slice_fusion.9), channel_id=1, source_target_pairs={{0,8},{1,9},{2,10},{3,11},{4,12},{5,13},{6,14},{7,15},{8,0},{9,1},... | collective-permute-start | bytes 393224 | tf_op jit(solution)/shard_map/ppermute | solution.py:24
  604.9 8.5 %collective-permute-start.68 = (bf16[4,1,2,64,128]{4,3,2,1,0:T(8,128)(2,1)S(1)}, bf16[4,1,2,64,128]{4,3,2,1,0:T(8,128)(2,1)S(1)}, u32[]{:S(2)}, u32[]{:S(2)}) collective-permute-start(bf16[4,1,2,64,128]{4,3,2,1,0:T(8,128)(2,1)S(1)} %constant_dynamic-slice_fusion.6), channel_id=1, source_target_pairs={{0,4},{1,5},{2,6},{3,7},{4,0},{5,1},{6,2},{7,3},{8,12},{9,13},{10,... | collective-permute-start | bytes 393224 | tf_op jit(solution)/shard_map/ppermute | solution.py:24
  613.4 11.8 %collective-permute-start.69 = (bf16[2,1,4,64,128]{4,3,2,1,0:T(8,128)(2,1)S(1)}, bf16[2,1,4,64,128]{4,3,2,1,0:T(8,128)(2,1)S(1)}, u32[]{:S(2)}, u32[]{:S(2)}) collective-permute-start(bf16[2,1,4,64,128]{4,3,2,1,0:T(8,128)(2,1)S(1)} %constant_dynamic-slice_fusion.5), channel_id=1, source_target_pairs={{0,8},{1,9},{2,10},{3,11},{4,12},{5,13},{6,14},{7,15},{8,0},{9,1},... | collective-permute-start | bytes 393224 | tf_op jit(solution)/shard_map/ppermute | solution.py:24
  630.8 9.1 %collective-permute-start.71 = (bf16[16,64,128]{2,1,0:T(8,128)(2,1)S(1)}, bf16[16,64,128]{2,1,0:T(8,128)(2,1)S(1)}, u32[]{:S(2)}, u32[]{:S(2)}) collective-permute-start(bf16[16,64,128]{2,1,0:T(8,128)(2,1)S(1)} %bitcast.345), channel_id=1, source_target_pairs={{0,32},{1,33},{2,34},{3,35},{4,36},{5,37},{6,38},{7,39},{8,40},{9,... | collective-permute-start | bytes 786440 | tf_op jit(solution)/shard_map/ppermute | solution.py:24
  658.2 10.3 %collective-permute-start.74 = (bf16[2,1,4,64,128]{4,3,2,1,0:T(8,128)(2,1)S(1)}, bf16[2,1,4,64,128]{4,3,2,1,0:T(8,128)(2,1)S(1)}, u32[]{:S(2)}, u32[]{:S(2)}) collective-permute-start(bf16[2,1,4,64,128]{4,3,2,1,0:T(8,128)(2,1)S(1)} %constant_dynamic-slice_fusion.1), channel_id=1, source_target_pairs={{0,8},{1,9},{2,10},{3,11},{4,12},{5,13},{6,14},{7,15},{8,0},{9,1},... | collective-permute-start | bytes 393224 | tf_op jit(solution)/shard_map/ppermute | solution.py:24
  (51 other events, 498.6 us)
